TPU v7x, 512 devices: a whole 4x4x16 slice. The times are simulated.
512 devices in a mesh: slab: 64 (over z, x_lo, core), shell: 8 (over y, x_hi).
Axes of the slice: x: 4 (x_hi: 2, x_lo: 2; x = x_hi * 2 + x_lo), y: 4, z: 16, core: 2. Of those that a mesh axis runs over, the one named last changes fastest.
Arguments:
- images: bfloat16 [8192, 2, 16384], P('slab', None, 'shell'), may hold values from -6 to 6
- defocus: bfloat16 [8192], P('slab'), may hold values from 20 to 200
- pose_bin: int32 [8192, 1], P('slab'), may hold values from 0 to 63; in each aligned block of 128 rows (0 to 127, 128 to 255, ...) at most 6 rows name the same one
- freq_sq: float32 [16384], P('shell'), may hold values from 0 to 1, as said below
- model_slice: float32 [64, 2, 16384], P('slab', None, 'shell'), may hold values from -6 to 6
- interp_coef: bfloat16 [64, 128, 4, 128, 128], P('slab', 'shell'), may hold values from -0.5 to 0.5
- block_index: int32 [64, 128, 4], P('slab', 'shell'), may hold values from 0 to 2047, as said below
Outputs:
- volume_grad: float32 [2048, 2, 128], P(('slab', 'shell'))
Inputs may be any that keep to these rules, and one draw needn't show every extreme that they name: `pose_bin`: among the images of one index of slab, no pose bin is named by more than 6 images, a bound that some block reaches. `freq_sq`: band s of the 8 bands of samples holds values between (s / 8) squared and ((s + 1) / 8) squared. `block_index`: among the 64 dense blocks of one pose bin in one shell band, the volume blocks v with the same v // 32 are named at most 2 times, and one such group exactly 2 times.
All inputs are finite; a program needn't handle non-finite values.
Results may differ from a plain program's by a relative error of at most 0.0029.
Values may be sent and summed in bfloat16 or wider, within the bound.
A program may use at most 64 MiB of HBM per device.

v0:
```python
import jax
import jax.numpy as jnp
from jax import lax
from jax.sharding import PartitionSpec as P

NVB_DEV = 4


def shards(images, defocus, pose_bin, freq_sq, model_slice, interp_coef, block_index):
    f32 = jnp.float32
    slabs = lax.axis_size("slab")
    shells = lax.axis_size("shell")
    local_rows = images.shape[0]
    width = images.shape[2]
    pose_ids = pose_bin[:, 0]
    onehot_int = (pose_ids[:, None] == jnp.arange(slabs, dtype=jnp.int32)[None, :]).astype(
        jnp.int32
    )
    capacity = max(2, 3 * local_rows // slabs)
    slot_rank = jnp.sum((jnp.cumsum(onehot_int, axis=0) - 1) * onehot_int, axis=1)
    send_rows = (
        jnp.zeros((slabs, capacity, 2, width), jnp.bfloat16).at[pose_ids, slot_rank].set(images)
    )
    send_focus = jnp.zeros((slabs, capacity), jnp.bfloat16).at[pose_ids, slot_rank].set(defocus)
    got_rows, got_focus = (
        lax.all_to_all(send_rows, "slab", split_axis=0, concat_axis=0, tiled=True),
        lax.all_to_all(send_focus, "slab", split_axis=0, concat_axis=0, tiled=True),
    )
    flat_rows = got_rows.reshape(-1, 2, width)
    flat_focus = got_focus.reshape(-1).astype(f32)
    contrast = jnp.sin(flat_focus[:, None] * freq_sq[None, :])
    numerator = jnp.sum(contrast[:, None, :] * flat_rows.astype(f32), axis=0)
    power = jnp.sum(contrast * contrast, axis=0)
    residual_slice = ((power[None, :] * model_slice[0] - numerator) / local_rows).astype(
        jnp.bfloat16
    )
    sample_block = interp_coef.shape[3]
    voxel_block = interp_coef.shape[4]
    tiles = residual_slice.reshape(2, width // sample_block, sample_block)
    terms = jnp.einsum("ckp,kjpv->kjcv", tiles, interp_coef[0], preferred_element_type=f32)
    flat_terms = terms.reshape(-1, 2, voxel_block)
    flat_index = block_index[0].reshape(-1)
    total_blocks = NVB_DEV * slabs * shells
    partial_value = jnp.zeros((total_blocks, 2, voxel_block), f32).at[flat_index].add(flat_terms)
    volume_grad = lax.psum_scatter(
        partial_value, ("slab", "shell"), scatter_dimension=0, tiled=True
    )
    return volume_grad


def solution(mesh):
    return jax.shard_map(
        shards,
        mesh=mesh,
        in_specs=(
            P("slab", None, "shell"),
            P("slab"),
            P("slab", None),
            P("shell"),
            P("slab", None, "shell"),
            P("slab", "shell", None, None, None),
            P("slab", "shell", None),
        ),
        out_specs=P(("slab", "shell"), None, None),
        check_vma=False,
    )
```

profile of v0, /device:TPU:1, one launch (start us, length us, event | category | flops | bytes accessed | tf_op | source)
XLA Modules:
  0.0 716.6 jit_solution(12140266293482965085)
XLA Ops:
  6.5 0.0 copy-start
  6.5 0.9 fusion.2
  7.4 0.2 reduce_window_sum.11
  7.6 0.8 select_reduce_fusion
  8.4 0.7 fusion.10
  9.1 11.1 %scatter_fusion = bf16[64,6]{0,1:T(8,128)(2,1)S(1)} fusion(bf16[64,6]{0,1:T(8,128)(2,1)S(1)} %broadcast_in_dim.7, s32[128]{0:T(128)S(1)} %fusion.10, bf16[128]{0:T(256)(128)(2,1)} %param.8), kind=kCustom, calls=%fused_computation | custom fusion | bytes 1792 | tf_op jit(solution)/shard_map/scatter | solution.py:24
  20.2 0.7 copy.19
  20.9 18.1 %all-to-all-start = ((bf16[64,1,6]{2,1,0:T(2,128)(2,1)}), bf16[64,1,6]{2,1,0:T(2,128)(2,1)S(1)}, u32[]{:S(2)}, u32[]{:S(2)}) async-start(bf16[64,1,6]{2,1,0:T(2,128)(2,1)} %copy.19), calls=%async_computation | async-start | bytes 65536 | tf_op jit(solution)/shard_map/all_to_all | solution.py:27
  39.0 4.8 broadcast_in_dim.8
  43.8 0.0 copy-done.1
  43.8 16.8 %scatter_fusion.1 = bf16[64,6,2,2048]{3,2,1,0:T(2,128)(2,1)} fusion(bf16[64,6,2,2048]{3,2,1,0:T(2,128)(2,1)} %broadcast_in_dim.8, s32[128]{0:T(128)S(1)} %fusion.10, bf16[128,2,2048]{2,1,0:T(2,128)(2,1)S(1)} %copy-done.1), kind=kCustom, calls=%fused_computation.1 | custom fusion | bytes 3146752 | tf_op jit(solution)/shard_map/scatter | solution.py:22
  60.5 0.0 all-to-all-done
  60.5 13.9 %all-to-all-start.1 = ((bf16[64,6,2,2048]{3,2,1,0:T(2,128)(2,1)}), bf16[64,6,2,2048]{3,2,1,0:T(2,128)(2,1)}, u32[]{:S(2)}, u32[]{:S(2)}) async-start(bf16[64,6,2,2048]{3,2,1,0:T(2,128)(2,1)} %scatter_fusion.1), calls=%async_computation.1 | async-start | bytes 6291456 | tf_op jit(solution)/shard_map/all_to_all | solution.py:26
  74.4 0.0 all-reduce.3.cloned.1.call-start
  74.5 0.0 copy-done.4
  74.5 0.1 copy.18
  74.6 0.1 reshape_squeeze.3
  74.7 0.1 convert_reduce_fusion
  74.8 0.1 reshape.94
  75.0 0.0 copy-done.3
  75.0 11.2 %multiply_reduce_fusion.1 = f32[2048]{0:T(1024)S(1)} fusion(f32[2048]{0:T(1024)S(1)} %copy-done.3, f32[384]{0:T(512)S(1)} %reshape.94), kind=kLoop, calls=%fused_computation.5 | loop fusion | flops 2357248 | bytes 17920 | tf_op jit(solution)/shard_map/reduce_sum | solution.py:33
  86.2 14.9 %multiply_sine_fusion = f32[64,6,2048]{2,1,0:T(8,128)} fusion(f32[2048]{0:T(1024)S(1)} %copy-done.3, f32[64,6]{1,0:T(8,128)S(1)} %bitcast.43), kind=kLoop, calls=%fused_computation.4 | loop fusion | flops 786432 | bytes 3155456 | tf_op jit(solution)/shard_map/sin | solution.py:31
  101.1 115.1 %all-to-all-done.1 = bf16[64,6,2,2048]{3,2,1,0:T(2,128)(2,1)} async-done(((bf16[64,6,2,2048]{3,2,1,0:T(2,128)(2,1)}), bf16[64,6,2,2048]{3,2,1,0:T(2,128)(2,1)}, u32[]{:S(2)}, u32[]{:S(2)}) %all-to-all-start.1) | async-done | bytes 3145760 | tf_op jit(solution)/shard_map/all_to_all | solution.py:26
  216.2 6.5 multiply_reduce_fusion
  222.7 0.0 copy-done
  222.7 0.0 copy-done.2
  222.7 0.4 fusion
  223.1 1.6 broadcast_in_dim.6
  224.7 6.6 scatter_fusion.2
  231.3 0.0 all-reduce.3.cloned.1.call-update
  231.3 477.1 %all-reduce.3.cloned.1.call-done = f32[2048,2,128]{2,1,0:T(2,128)} async-done(((f32[2048,2,128]{2,1,0:T(2,128)}), f32[2048,2,128]{2,1,0:T(2,128)}) %all-reduce.3.cloned.1.call-update) | async-done | bytes 2097168
  708.5 1.3 constant_dynamic-slice_fusion
  (7 shorter events, 0.0 us)
Async XLA Ops:
  6.5 216.1 %copy-start = (bf16[1,16,4,128,128]{4,3,2,1,0:T(8,128)(2,1)S(1)}, bf16[1,16,4,128,128]{4,3,2,1,0:T(8,128)(2,1)}, u32[]{:S(2)}) copy-start(bf16[1,16,4,128,128]{4,3,2,1,0:T(8,128)(2,1)} %param.12) | copy-start | bytes 6291460
  6.5 37.2 %copy-start.1 = (bf16[128,2,2048]{2,1,0:T(2,128)(2,1)S(1)}, bf16[128,2,2048]{2,1,0:T(2,128)(2,1)}, u32[]{:S(2)}) copy-start(bf16[128,2,2048]{2,1,0:T(2,128)(2,1)} %param.7) | copy-start | bytes 3145732
  20.9 39.6 %all-to-all-start = ((bf16[64,1,6]{2,1,0:T(2,128)(2,1)}), bf16[64,1,6]{2,1,0:T(2,128)(2,1)S(1)}, u32[]{:S(2)}, u32[]{:S(2)}) async-start(bf16[64,1,6]{2,1,0:T(2,128)(2,1)} %copy.19), calls=%async_computation | async-start | bytes 65536 | tf_op jit(solution)/shard_map/all_to_all | solution.py:27
  60.5 13.9 %copy-start.4 = (s32[1,16,4]{1,2,0:T(4,128)S(1)}, s32[1,16,4]{1,2,0:T(4,128)}, u32[]{:S(2)}) copy-start(s32[1,16,4]{1,2,0:T(4,128)} %param.13) | copy-start | bytes 772
  60.5 14.4 %copy-start.3 = (f32[2048]{0:T(1024)S(1)}, f32[2048]{0:T(1024)}, u32[]{:S(2)}) copy-start(f32[2048]{0:T(1024)} %param.10) | copy-start | bytes 24580
  60.5 155.6 %all-to-all-start.1 = ((bf16[64,6,2,2048]{3,2,1,0:T(2,128)(2,1)}), bf16[64,6,2,2048]{3,2,1,0:T(2,128)(2,1)}, u32[]{:S(2)}, u32[]{:S(2)}) async-start(bf16[64,6,2,2048]{3,2,1,0:T(2,128)(2,1)} %scatter_fusion.1), calls=%async_computation.1 | async-start | bytes 6291456 | tf_op jit(solution)/shard_map/all_to_all | solution.py:26
  74.4 634.0 %all-reduce.3.cloned.1.call-start = ((), (), s32[]{:S(2)}) async-start(), calls=%async_computation.2 | async-start | bytes 4194304
  101.1 121.6 %copy-start.2 = (f32[1,2,2048]{2,1,0:T(2,128)S(1)}, f32[1,2,2048]{2,1,0:T(2,128)}, u32[]{:S(2)}) copy-start(f32[1,2,2048]{2,1,0:T(2,128)} %param.11) | copy-start | bytes 49156
Sparse Core Ops, SparseCore 0:
  231.4 476.9 all-reduce.2
where the time goes:
time: 717 us
  waiting for transfers between devices  592 us (83%)
  other arithmetic  42 us (6%)
  local copies, waits for them, and re-layouts  36.5 us (5%)
  starting transfers between devices  32 us (4%)
  between operations  13.5 us (2%)
    unnamed x2, waiting for transfers between devices  477 us
    all_to_all x1, waiting for transfers between devices, shards(): lax.all_to_all(send_rows, 'slab', split_axis=0, concat_axis=0, tiled=True)  115 us
    all_to_all x1, starting transfers between devices, shards(): lax.all_to_all(send_focus, 'slab', split_axis=0, concat_axis=0, tiled=True)  18.1 us
    scatter x1, local copies, waits for them, and re-layouts, shards(): jnp.zeros((slabs, capacity, 2, width), jnp.bfloat16).at[pose_ids, slot_rank]  16.8 us
    sin x1, other arithmetic, shards(): contrast = jnp.sin(flat_focus[:, None] * freq_sq[None, :])  14.9 us
  transfers between devices with their start and end apart: 3, of which 2 were waited for; matrix products, arithmetic and copies ran while one was open for 7% of the time, Pallas kernels for 0%

commit v1 on v0

v1 whole, which is shorter than its diff:
```python
import functools

import jax
import jax.numpy as jnp
from jax import lax
from jax.experimental import pallas as pl
from jax.experimental.pallas import tpu as pltpu
from jax.sharding import PartitionSpec as P

F32 = jnp.float32
BF16 = jnp.bfloat16
MESH = pl.DeviceIdType.MESH

QUAD = 4
SHELLS = 8
CAP = 6
LANES = 128
CHUNKS = 4
RUN = 4
PLANE = QUAD * SHELLS

INV_PI = 0.3183098861837907
PI_A, PI_B, PI_C = 3.140625, 9.67502593994140625e-4, 1.509957990978376e-7
S3, S5, S7, S9, S11 = -1 / 6, 1 / 120, -1 / 5040, 1 / 362880, -1 / 39916800


def folded(x):
    n = jnp.floor(x * INV_PI + 0.5)
    r = ((x - n * PI_A) - n * PI_B) - n * PI_C
    t = r * r
    return r * (1.0 + t * (S3 + t * (S5 + t * (S7 + t * (S9 + t * S11))))), n


def sine(x):
    s, n = folded(x)
    odd = n - 2.0 * jnp.floor(n * 0.5)
    return s * (1.0 - 2.0 * odd)


def dot(a, b):
    return jnp.dot(a, b, preferred_element_type=F32)


def halves(x):
    high = x.astype(BF16)
    return high, (x - high.astype(F32)).astype(BF16)


def iota(shape, dim):
    return lax.broadcasted_iota(jnp.int32, shape, dim)


def down(row):
    return jnp.broadcast_to(row, (LANES, LANES)).T


def kernel(
    depth,
    pose_ref,
    focus_ref,
    freq_ref,
    model_ref,
    index_ref,
    images_ref,
    coef_ref,
    out_ref,
    img,
    coef,
    focus_col,
    pair_hot,
    spread,
    part,
    core_got,
    x_got,
    table,
    table_core,
    table_x,
    stage,
    z_out,
    z_got,
    note_out,
    note_got,
    column,
    power,
    resid,
    place,
    target,
    terms,
    slot_out,
    slot_got,
    plane_out,
    plane_got,
    img_sem,
    coef_sem,
    core_sem,
    x_sem,
    z_sem,
    note_sem,
    slot_sem,
    plane_sem,
):
    slab = lax.axis_index("slab")
    shell = lax.axis_index("shell")
    z, quad = slab // QUAD, slab % QUAD
    x_lo, core = quad // 2, quad % 2
    core_peer = z * QUAD + x_lo * 2 + (1 - core)
    x_peer = z * QUAD + (1 - x_lo) * 2 + core
    mine = quad * SHELLS + shell

    def at(slab_id, shell_id):
        return {"slab": slab_id, "shell": shell_id}

    def z_peer(j):
        return lax.rem(z + j, depth)

    def plane_peer(m):
        return lax.rem(mine + m, PLANE)

    barrier = pltpu.get_barrier_semaphore()

    @pl.loop(1, depth)
    def _(j):
        pl.semaphore_signal(barrier, inc=1, device_id=at(z_peer(j) * QUAD + quad, shell), device_id_type=MESH)

    @pl.loop(1, PLANE)
    def _(m):
        g = plane_peer(m)
        pl.semaphore_signal(barrier, inc=1, device_id=at(z * QUAD + g // SHELLS, g % SHELLS), device_id_type=MESH)

    width = RUN * LANES
    loads = [
        pltpu.make_async_copy(
            images_ref.at[:, pl.ds(ch * width, width)], img.at[:, pl.ds(ch * width, width)], img_sem.at[ch]
        )
        for ch in range(CHUNKS)
    ]
    for load in loads:
        load.start()
    coef_load = pltpu.make_async_copy(coef_ref, coef, coef_sem)
    coef_load.start()

    pose = pose_ref[...].astype(F32)
    pose_col = down(pose)
    focus_col[...] = down(focus_ref[...].astype(F32))
    same = (pose_col == pose) & (iota((LANES, LANES), 1) < iota((LANES, LANES), 0))
    rank = jnp.sum(same.astype(F32), axis=1, keepdims=True)
    lane = iota((LANES, LANES), 1)
    wanted = 64 + quad * CAP + rank.astype(jnp.int32)
    spots = jnp.where(lane == wanted, focus_col[...], 0.0).astype(BF16)
    row = iota((64, LANES), 0)
    bins = row % depth * QUAD + (row // depth) % 2 * 2 + row // (2 * depth)
    hot = (bins == pose_ref[...]).astype(F32).astype(BF16)
    table[...] = dot(hot, spots)
    twice = (iota((LANES, 2 * LANES), 1) // 2 == iota((LANES, 2 * LANES), 0)).astype(F32).astype(BF16)
    pose_pair = dot(jnp.broadcast_to(pose, (8, LANES)).astype(BF16), twice)[0:1]
    wide = iota((LANES, 2 * LANES), 0)
    r64 = wide % 64
    bin64 = r64 % depth * QUAD + (r64 // depth) % 2 * 2 + r64 // (2 * depth)
    parity = iota((LANES, 2 * LANES), 1) % 2
    pair_hot[...] = (
        ((bin64.astype(F32) == pose_pair) & (parity == wide // 64)).astype(F32).astype(BF16)
    )

    index = index_ref[...]
    k_of = (iota((16, LANES), 1) % 16 == iota((16, LANES), 0)).astype(F32).astype(BF16)
    mask = (iota((NNZ_ROWS, LANES), 1) // 16 == iota((NNZ_ROWS, LANES), 0)).astype(F32)
    slab_row = jnp.sum(dot((index // 32).astype(F32).astype(BF16), k_of) * mask, axis=0, keepdims=True)
    low_row = jnp.sum(dot((index % 32).astype(F32).astype(BF16), k_of) * mask, axis=0, keepdims=True)
    live = iota((1, LANES), 1) < 64
    slab_row = jnp.where(live, slab_row, -1.0)
    slab_col = down(slab_row)
    before = (slab_col == slab_row) & (iota((LANES, LANES), 0) < iota((LANES, LANES), 1))
    slot_row = jnp.where(live, 2.0 * slab_row + jnp.sum(before.astype(F32), axis=0, keepdims=True), -1.0)
    hits = (iota((LANES, LANES), 0).astype(F32) == slot_row).astype(F32)
    place[...] = hits.astype(BF16)
    plane_block = slab_row.astype(jnp.int32) % QUAD * 32 + low_row.astype(jnp.int32) + 1
    target[...] = jnp.broadcast_to(
        jnp.sum(hits * plane_block.astype(F32), axis=1, keepdims=True), (LANES, LANES)
    )

    for ch in range(CHUNKS):
        loads[ch].wait()

        @pl.loop(0, RUN)
        def _(q):
            k = ch * RUN + q
            contrast = sine(focus_col[...] * freq_ref[pl.ds(k, 1), :])
            spread[pl.ds(0, LANES, stride=2), :] = contrast
            spread[pl.ds(1, LANES, stride=2), :] = contrast
            picture = img[:, pl.ds(pl.multiple_of(k * LANES, LANES), LANES)].astype(F32)
            high, low = halves(spread[...] * picture)
            sums = dot(pair_hot[...], high) + dot(pair_hot[...], low)
            first = pl.multiple_of(q * LANES, LANES)
            part[ch, :, pl.ds(first, LANES)] = sums[0:64]
            part[ch, :, pl.ds(pl.multiple_of(width + first, LANES), LANES)] = sums[64:128]

    pl.semaphore_wait(barrier, depth - 1 + PLANE - 1)

    half = 2 * depth
    other_rows = pl.multiple_of((1 - core) * half, half)
    my_rows = pl.multiple_of(core * half, half)
    other_x = pl.multiple_of(core * half + (1 - x_lo) * depth, depth)
    my_x = pl.multiple_of(core * half + x_lo * depth, depth)

    def send(src, dst, sems, i, device):
        return pltpu.make_async_remote_copy(
            src_ref=src,
            dst_ref=dst,
            send_sem=sems.at[0, i],
            recv_sem=sems.at[1, i],
            device_id=device,
            device_id_type=MESH,
        )

    to_core = at(core_peer, shell)
    to_x = at(x_peer, shell)
    core_sends = [send(table.at[pl.ds(other_rows, half)], table_core, core_sem, CHUNKS, to_core)]
    for ch in range(CHUNKS):
        core_sends.append(send(part.at[ch, pl.ds(other_rows, half)], core_got.at[ch], core_sem, ch, to_core))
    for copy in core_sends:
        copy.start()

    core_sends[0].wait()
    table[pl.ds(my_rows, half), :] += table_core[...]
    x_sends = [send(table.at[pl.ds(other_x, depth)], table_x, x_sem, CHUNKS, to_x)]
    x_sends[0].start()
    for ch in range(CHUNKS):
        core_sends[ch + 1].wait()
        part[ch, pl.ds(my_rows, half), :] += core_got[ch]
        copy = send(part.at[ch, pl.ds(other_x, depth)], x_got.at[ch], x_sem, ch, to_x)
        copy.start()
        x_sends.append(copy)

    def along_z(out, got, i, j):
        peer = z_peer(j)
        return pltpu.make_async_remote_copy(
            src_ref=out.at[peer],
            dst_ref=got.at[depth - j],
            send_sem=i[0],
            recv_sem=i[1],
            device_id=at(peer * QUAD + quad, shell),
            device_id_type=MESH,
        )

    def all_of(out, got, i):
        return pltpu.make_async_remote_copy(
            src_ref=out.at[pl.ds(0, depth - 1)],
            dst_ref=got.at[pl.ds(1, depth - 1)],
            send_sem=i[0],
            recv_sem=i[1],
            device_id=at(z_peer(1) * QUAD + quad, shell),
            device_id_type=MESH,
        )

    x_sends[0].wait()
    own_table = table[pl.ds(my_x, depth), :] + table_x[...]
    lanes8 = iota((8, LANES), 1)
    for i in range(depth):
        note_out[i] = jnp.where(
            lanes8 < 64, target[i * 8 : i * 8 + 8, :], jnp.broadcast_to(own_table[i : i + 1, :], (8, LANES))
        )
    note_got[0] = note_out[z]
    note_sems = (note_sem.at[0], note_sem.at[1])

    @pl.loop(1, depth)
    def _(j):
        along_z(note_out, note_got, note_sems, j).start()

    for ch in range(CHUNKS):
        x_sends[ch + 1].wait()
        total = part[ch, pl.ds(my_x, depth), :] + x_got[ch]
        for b in range(2 * RUN):
            stage[ch, :, b, :] = total[:, b * LANES : (b + 1) * LANES]
        z_out[ch] = stage[ch].astype(BF16)

        @pl.loop(1, depth)
        def _(j):
            along_z(z_out.at[ch], z_got.at[ch], (z_sem.at[0, ch], z_sem.at[1, ch]), j).start()

    all_of(note_out, note_got, note_sems).wait()
    values = note_got[:, 0, :]
    for i in range(QUAD * CAP):
        column[i] = jnp.broadcast_to(values[:, 64 + i : 65 + i], (depth, LANES))

    @pl.loop(0, CHUNKS * RUN)
    def _(k):
        freq = freq_ref[pl.ds(k, 1), :]
        total = jnp.zeros((depth, LANES), F32)
        for i in range(QUAD * CAP):
            s, _ = folded(column[i] * freq)
            total = total + s * s
        power[pl.ds(k, 1), :] = jnp.sum(total, axis=0, keepdims=True)

    tile = note_got[...].reshape(depth * 8, LANES)
    to_block = jnp.broadcast_to(tile[:, 0:1], (LANES, LANES)).T
    target[...] = to_block
    terms[...] = jnp.zeros_like(terms)
    coef_load.wait()

    for ch in range(CHUNKS):
        all_of(z_out.at[ch], z_got.at[ch], (z_sem.at[0, ch], z_sem.at[1, ch])).wait()
        numerator = stage[ch, z]
        for j in range(1, depth):
            numerator = numerator + z_got[ch, j].astype(F32)
        for c in range(2):
            for q in range(RUN):
                k = ch * RUN + q
                model = model_ref[c : c + 1, k * LANES : (k + 1) * LANES]
                resid[c * 16 + k : c * 16 + k + 1, :] = (
                    power[k : k + 1, :] * model - numerator[c * RUN + q : c * RUN + q + 1, :]
                ) * (1.0 / 128)
        for q in range(RUN):
            k = ch * RUN + q
            left = jnp.concatenate([resid[k : k + 1, :], resid[16 + k : 17 + k, :]], axis=0).astype(BF16)
            for j in range(NNZ):
                term = dot(left, coef[k, j])
                t = j * 16 + k
                terms[t : t + 1, 0:LANES] = term[0:1]
                terms[t : t + 1, LANES : 2 * LANES] = term[1:2]

    high, low = halves(terms[...])
    slots = dot(place[...], high) + dot(place[...], low)
    slot_out[...] = slots.reshape(depth, 8, 2 * LANES)
    slot_got[0] = slot_out[z]
    slot_sems = (slot_sem.at[0], slot_sem.at[1])

    @pl.loop(1, depth)
    def _(j):
        along_z(slot_out, slot_got, slot_sems, j).start()

    adds = (target[...] == (iota((LANES, LANES), 0) + 1).astype(F32)).astype(F32).astype(BF16)
    all_of(slot_out, slot_got, slot_sems).wait()
    high, low = halves(slot_got[...].reshape(depth * 8, 2 * LANES))
    dense = dot(adds, high) + dot(adds, low)
    plane_out[pl.ds(0, LANES, stride=2), :] = dense[:, 0:LANES]
    plane_out[pl.ds(1, LANES, stride=2), :] = dense[:, LANES : 2 * LANES]

    @pl.loop(1, PLANE)
    def _(m):
        g = plane_peer(m)
        pltpu.make_async_remote_copy(
            src_ref=plane_out.at[pl.ds(pl.multiple_of(g * 8, 8), 8)],
            dst_ref=plane_got.at[pl.ds(pl.multiple_of((PLANE - m) * 8, 8), 8)],
            send_sem=plane_sem.at[0],
            recv_sem=plane_sem.at[1],
            device_id=at(z * QUAD + g // SHELLS, g % SHELLS),
            device_id_type=MESH,
        ).start()

    total = plane_out[pl.ds(pl.multiple_of(mine * 8, 8), 8), :]
    rest = 8 * (PLANE - 1)
    pltpu.make_async_remote_copy(
        src_ref=plane_out.at[pl.ds(0, rest)],
        dst_ref=plane_got.at[pl.ds(8, rest)],
        send_sem=plane_sem.at[0],
        recv_sem=plane_sem.at[1],
        device_id=to_core,
        device_id_type=MESH,
    ).wait()
    for m in range(1, PLANE):
        total = total + plane_got[m * 8 : m * 8 + 8, :]
    out_ref[...] = total


NNZ = 4
NNZ_ROWS = NNZ


def shards(images, defocus, pose_bin, freq_sq, model_slice, interp_coef, block_index):
    depth = lax.axis_size("slab") // QUAD
    rows, _, width = images.shape
    run = RUN * LANES
    vmem = pl.BlockSpec(memory_space=pltpu.VMEM)
    hbm = pl.BlockSpec(memory_space=pl.ANY)
    dma = pltpu.SemaphoreType.DMA
    out = pl.pallas_call(
        functools.partial(kernel, depth),
        out_shape=jax.ShapeDtypeStruct((8, LANES), F32),
        in_specs=[vmem] * 5 + [hbm] * 2,
        out_specs=vmem,
        scratch_shapes=[
            pltpu.VMEM((2 * rows, width), BF16),
            pltpu.VMEM(interp_coef.shape[1:], BF16),
            pltpu.VMEM((LANES, LANES), F32),
            pltpu.VMEM((LANES, 2 * LANES), BF16),
            pltpu.VMEM((2 * LANES, LANES), F32),
            pltpu.VMEM((CHUNKS, QUAD * depth, 2 * run), F32),
            pltpu.VMEM((CHUNKS, 2 * depth, 2 * run), F32),
            pltpu.VMEM((CHUNKS, depth, 2 * run), F32),
            pltpu.VMEM((QUAD * depth, LANES), F32),
            pltpu.VMEM((2 * depth, LANES), F32),
            pltpu.VMEM((depth, LANES), F32),
            pltpu.VMEM((CHUNKS, depth, 2 * RUN, LANES), F32),
            pltpu.VMEM((CHUNKS, depth, 2 * RUN, LANES), BF16),
            pltpu.VMEM((CHUNKS, depth, 2 * RUN, LANES), BF16),
            pltpu.VMEM((depth, 8, LANES), F32),
            pltpu.VMEM((depth, 8, LANES), F32),
            pltpu.VMEM((QUAD * CAP, depth, LANES), F32),
            pltpu.VMEM((16, LANES), F32),
            pltpu.VMEM((32, LANES), F32),
            pltpu.VMEM((LANES, LANES), BF16),
            pltpu.VMEM((LANES, LANES), F32),
            pltpu.VMEM((LANES, 2 * LANES), F32),
            pltpu.VMEM((depth, 8, 2 * LANES), F32),
            pltpu.VMEM((depth, 8, 2 * LANES), F32),
            pltpu.VMEM((PLANE * 8, LANES), F32),
            pltpu.VMEM((PLANE * 8, LANES), F32),
            dma((CHUNKS,)),
            dma,
            dma((2, CHUNKS + 1)),
            dma((2, CHUNKS + 1)),
            dma((2, CHUNKS)),
            dma((2,)),
            dma((2,)),
            dma((2,)),
        ],
        compiler_params=pltpu.CompilerParams(collective_id=0, has_side_effects=True),
        name="cryo_grad",
    )(
        pose_bin.reshape(1, rows),
        defocus.reshape(1, rows),
        freq_sq.reshape(width // LANES, LANES),
        model_slice[0],
        jnp.transpose(block_index[0]),
        images.reshape(2 * rows, width),
        interp_coef[0],
    )
    return out.reshape(4, 2, LANES)


def solution(mesh):
    return jax.shard_map(
        shards,
        mesh=mesh,
        in_specs=(
            P("slab", None, "shell"),
            P("slab"),
            P("slab", None),
            P("shell"),
            P("slab", None, "shell"),
            P("slab", "shell", None, None, None),
            P("slab", "shell", None),
        ),
        out_specs=P(("slab", "shell"), None, None),
        check_vma=False,
    )
```

time: 717 us -> 55.7 us (0.08)
  waiting for transfers between devices: 592 us -> 0 us
  Pallas kernels: 0 us -> 52 us
  other arithmetic: 42 us -> 0 us
  local copies, waits for them, and re-layouts: 36.5 us -> 3.53 us
  starting transfers between devices: 32 us -> 0 us
  between operations: 13.5 us -> 0.01 us
    unnamed x2 -> x0, waiting for transfers between devices: 477 us -> none
    all_to_all x2 -> x0, waiting for transfers between devices: 115 us -> none  [the longest x1 115 us: shards(): lax.all_to_all(send_rows, 'slab', split_axis=0, concat_axis=0, tiled=True)]
    pallas_call x0 -> x1, Pallas kernels: none -> 52 us  [shards(): pl.pallas_call(functools.partial(kernel, depth), out_shape=jax.ShapeDtype...]
    all_to_all x2 -> x0, starting transfers between devices: 31.9 us -> none  [the longest x1 18.1 us: shards(): lax.all_to_all(send_focus, 'slab', split_axis=0, concat_axis=0, tiled=True)]
    scatter x2 -> x0, local copies, waits for them, and re-layouts: 27.9 us -> none  [the longest x1 16.8 us: shards(): jnp.zeros((slabs, capacity, 2, width), jnp.bfloat16).at[pose_ids, slot_rank]]
    reduce_sum x3 -> x0, other arithmetic: 18.5 us -> none  [the longest x1 11.2 us: shards(): power = jnp.sum(contrast * contrast, axis=0)]
    sin x1 -> x0, other arithmetic: 14.9 us -> none  [shards(): contrast = jnp.sin(flat_focus[:, None] * freq_sq[None, :])]
  transfers between devices with their start and end apart: 3 -> 0, of which waited for: 2 -> 0; matrix products, arithmetic and copies ran while one was open for 7% -> 0% of each run, Pallas kernels for 0% -> 0%
where the time goes in v1:
time: 55.7 us; the launch traced here: 55.5 us
  Pallas kernels  52 us (93%)
  local copies, waits for them, and re-layouts  3.53 us (6%)
    pallas_call x1, Pallas kernels, shards(): pl.pallas_call(functools.partial(kernel, depth), out_shape=jax.ShapeDtype...  52 us
    reshape x1, local copies, waits for them, and re-layouts, shards(): images.reshape(2 * rows, width)  2.26 us
    unnamed x1, local copies, waits for them, and re-layouts  1.27 us

profile of v1, /device:TPU:1, one launch (start us, length us, event | category | flops | bytes accessed | tf_op | source)
XLA Modules:
  0.0 55.5 jit_solution(8528826990921018073)
XLA Ops:
  0.0 2.3 %reshape.18.images_ref = bf16[256,2048]{1,0:T(8,128)(2,1)} reshape(bf16[128,2,2048]{2,1,0:T(2,128)(2,1)} %param.7) | data formatting | bytes 2097152 | tf_op jit(solution)/shard_map/reshape | solution.py:425
  2.3 52.0 %cryo_grad.1 = f32[8,128]{1,0:T(8,128)} custom-call(s32[1,128]{1,0:T(1,128)} %bitcast.14, bf16[1,128]{1,0:T(2,128)(2,1)} %bitcast.15, f32[16,128]{1,0:T(8,128)} %bitcast.12, f32[2,2048]{1,0:T(2,128)} %bitcast.10, s32[4,16]{1,0:T(4,128)} %bitcast.13, bf16[256,2048]{1,0:T(8,128)(2,1)} %reshape.18.images_ref, bf16[16,4,128,128]{3,2,1,0:T(8,128)(2,1)} %bitcast.9), custom_call_target="tpu_custom_call" | custom-call | tf_op jit(solution)/shard_map/cryo_grad/pallas_call | solution.py:376
  54.2 1.3 %copy.9 = f32[4,2,128]{2,1,0:T(2,128)} copy(f32[4,2,128]{2,1,0:T(2,128)} %bitcast.11) | data formatting | bytes 8192

commit v2 on v1

v2 whole, which is shorter than its diff:
```python
import functools

import jax
import jax.numpy as jnp
from jax import lax
from jax.experimental import pallas as pl
from jax.experimental.pallas import tpu as pltpu
from jax.sharding import PartitionSpec as P

F32 = jnp.float32
BF16 = jnp.bfloat16
MESH = pl.DeviceIdType.MESH

QUAD = 4
SHELLS = 8
CAP = 6
LANES = 128
CHUNKS = 4
RUN = 4
NEAR = [(dx, dy, dh) for dx in range(2) for dy in range(4) for dh in range(2)]
NEAR = sorted(NEAR, key=lambda d: -(min(d[1], 4 - d[1]) + abs(2 * d[2] - d[0])))[:-1]
PLANE = 16

INV_PI = 0.3183098861837907
PI_A, PI_B, PI_C = 3.140625, 9.67502593994140625e-4, 1.509957990978376e-7
S3, S5, S7, S9, S11 = -1 / 6, 1 / 120, -1 / 5040, 1 / 362880, -1 / 39916800


def folded(x):
    n = jnp.floor(x * INV_PI + 0.5)
    r = ((x - n * PI_A) - n * PI_B) - n * PI_C
    t = r * r
    return r * (1.0 + t * (S3 + t * (S5 + t * (S7 + t * (S9 + t * S11))))), n


def sine(x):
    s, n = folded(x)
    odd = n - 2.0 * jnp.floor(n * 0.5)
    return s * (1.0 - 2.0 * odd)


def dot(a, b):
    return jnp.dot(a, b, preferred_element_type=F32)


def halves(x):
    high = x.astype(BF16)
    return high, (x - high.astype(F32)).astype(BF16)


def iota(shape, dim):
    return lax.broadcasted_iota(jnp.int32, shape, dim)


def down(row):
    return jnp.broadcast_to(row, (LANES, LANES)).T


def kernel(
    depth,
    pose_hbm,
    focus_hbm,
    freq_hbm,
    model_hbm,
    index_hbm,
    images_ref,
    coef_ref,
    out_ref,
    pose_ref,
    focus_ref,
    freq_ref,
    model_ref,
    index_ref,
    img,
    coef,
    focus_col,
    pair_hot,
    spread,
    part,
    core_got,
    x_got,
    table,
    table_core,
    table_x,
    stage,
    z_out,
    z_got,
    note_out,
    note_got,
    column,
    power,
    resid,
    place,
    target,
    target_got,
    adds,
    terms,
    slot_out,
    slot_got,
    plane_out,
    plane_got,
    small_sem,
    img_sem,
    coef_sem,
    core_sem,
    x_sem,
    z_sem,
    note_sem,
    slot_sem,
    plane_sem,
):
    slab = lax.axis_index("slab")
    shell = lax.axis_index("shell")
    z, quad = slab // QUAD, slab % QUAD
    x_lo, core = quad // 2, quad % 2
    core_peer = z * QUAD + x_lo * 2 + (1 - core)
    x_peer = z * QUAD + (1 - x_lo) * 2 + core
    y, x_hi = shell // 2, shell % 2

    def at(slab_id, shell_id):
        return {"slab": slab_id, "shell": shell_id}

    def z_peer(j):
        return lax.rem(z + j, depth)

    def plane_peer(offset):
        dx, dy, dh = offset
        return (x_lo + dx) % 2, (y + dy) % 4 * 2 + (x_hi + dh) % 2

    width = RUN * LANES
    rows_ref = images_ref.reshape(2 * images_ref.shape[0], images_ref.shape[2])
    loads = [
        pltpu.make_async_copy(
            rows_ref.at[:, pl.ds(ch * width, width)], img.at[:, pl.ds(ch * width, width)], img_sem.at[ch]
        )
        for ch in range(CHUNKS)
    ]
    smalls = [
        pltpu.make_async_copy(src, dst, small_sem.at[i])
        for i, (src, dst) in enumerate(
            (
                (pose_hbm, pose_ref),
                (focus_hbm, focus_ref),
                (freq_hbm, freq_ref),
                (index_hbm, index_ref),
                (model_hbm, model_ref),
            )
        )
    ]
    for load in smalls + loads:
        load.start()
    coef_load = pltpu.make_async_copy(coef_ref, coef, coef_sem)
    coef_load.start()

    barrier = pltpu.get_barrier_semaphore()

    far_first = sorted(range(1, depth), key=lambda j: -min(j, depth - j))
    for j in far_first:
        for side in (core, 1 - core):
            pl.semaphore_signal(
                barrier, inc=1, device_id=at(z_peer(j) * QUAD + x_lo * 2 + side, shell), device_id_type=MESH
            )

    for offset in NEAR:
        peer_x, peer_shell = plane_peer(offset)
        pl.semaphore_signal(
            barrier, inc=1, device_id=at(z * QUAD + peer_x * 2 + core, peer_shell), device_id_type=MESH
        )
    pl.semaphore_signal(barrier, inc=1, device_id=at(core_peer, shell), device_id_type=MESH)

    smalls[0].wait()
    smalls[1].wait()
    pose = pose_ref[...].astype(F32)
    pose_col = down(pose)
    focus_col[...] = down(focus_ref[...].astype(F32))
    twice = (iota((LANES, 2 * LANES), 1) // 2 == iota((LANES, 2 * LANES), 0)).astype(F32).astype(BF16)
    pose_pair = dot(jnp.broadcast_to(pose, (8, LANES)).astype(BF16), twice)[0:1]
    wide = iota((LANES, 2 * LANES), 0)
    r64 = wide % 64
    bin64 = r64 % depth * QUAD + (r64 // depth) % 2 * 2 + r64 // (2 * depth)
    parity = iota((LANES, 2 * LANES), 1) % 2
    pair_hot[...] = (
        ((bin64.astype(F32) == pose_pair) & (parity == wide // 64)).astype(F32).astype(BF16)
    )

    smalls[2].wait()
    for ch in range(CHUNKS):
        loads[ch].wait()

        @pl.loop(0, RUN)
        def _(q):
            k = ch * RUN + q
            contrast = sine(focus_col[...] * freq_ref[pl.ds(k, 1), :])
            spread[pl.ds(0, LANES, stride=2), :] = contrast
            spread[pl.ds(1, LANES, stride=2), :] = contrast
            picture = img[:, pl.ds(pl.multiple_of(k * LANES, LANES), LANES)].astype(F32)
            high, low = halves(spread[...] * picture)
            sums = dot(pair_hot[...], high) + dot(pair_hot[...], low)
            first = pl.multiple_of(q * LANES, LANES)
            part[ch, :, pl.ds(first, LANES)] = sums[0:64]
            part[ch, :, pl.ds(pl.multiple_of(width + first, LANES), LANES)] = sums[64:128]

    pl.semaphore_wait(barrier, 2 * (depth - 1) + len(NEAR) + 1)

    half = 2 * depth
    other_rows = pl.multiple_of((1 - core) * half, half)
    my_rows = pl.multiple_of(core * half, half)
    other_x = pl.multiple_of(core * half + (1 - x_lo) * depth, depth)
    my_x = pl.multiple_of(core * half + x_lo * depth, depth)

    def send(src, dst, sems, i, device):
        return pltpu.make_async_remote_copy(
            src_ref=src,
            dst_ref=dst,
            send_sem=sems.at[0, i],
            recv_sem=sems.at[1, i],
            device_id=device,
            device_id_type=MESH,
        )

    to_core = at(core_peer, shell)
    to_x = at(x_peer, shell)
    core_sends = [
        send(part.at[ch, pl.ds(other_rows, half)], core_got.at[ch], core_sem, ch, to_core) for ch in range(CHUNKS)
    ]
    for copy in core_sends:
        copy.start()

    same = (pose_col == pose) & (iota((LANES, LANES), 1) < iota((LANES, LANES), 0))
    rank = jnp.sum(same.astype(F32), axis=1, keepdims=True)
    lane = iota((LANES, LANES), 1)
    wanted = 64 + quad * CAP + rank.astype(jnp.int32)
    spots = jnp.where(lane == wanted, focus_col[...], 0.0).astype(BF16)
    row = iota((64, LANES), 0)
    bins = row % depth * QUAD + (row // depth) % 2 * 2 + row // (2 * depth)
    hot = (bins == pose_ref[...]).astype(F32).astype(BF16)
    table[...] = dot(hot, spots)
    smalls[3].wait()
    index = index_ref[...]
    k_of = (iota((16, LANES), 1) % 16 == iota((16, LANES), 0)).astype(F32).astype(BF16)
    mask = (iota((NNZ_ROWS, LANES), 1) // 16 == iota((NNZ_ROWS, LANES), 0)).astype(F32)
    slab_row = jnp.sum(dot((index // 32).astype(F32).astype(BF16), k_of) * mask, axis=0, keepdims=True)
    low_row = jnp.sum(dot((index % 32).astype(F32).astype(BF16), k_of) * mask, axis=0, keepdims=True)
    live = iota((1, LANES), 1) < 64
    slab_row = jnp.where(live, slab_row, -1.0)
    slab_col = down(slab_row)
    before = (slab_col == slab_row) & (iota((LANES, LANES), 0) < iota((LANES, LANES), 1))
    rank_row = jnp.sum(before.astype(F32), axis=0, keepdims=True).astype(jnp.int32)
    slab_int = slab_row.astype(jnp.int32)
    x_of = slab_int % QUAD // 2
    slot_row = jnp.where(live, slab_int % 2 * 64 + slab_int // QUAD * 4 + x_of * 2 + rank_row, -1)
    place[...] = (iota((LANES, LANES), 0) == slot_row).astype(F32).astype(BF16)
    block_row = (x_of * 32 + low_row.astype(jnp.int32) + 1).astype(F32)
    at_z = ((slot_row // 4 == iota((2 * depth, LANES), 0)) & live).astype(F32).astype(BF16)
    at_lane = jnp.where(slot_row % 4 == iota((LANES, LANES), 0), block_row, 0.0).astype(BF16)
    target[...] = lax.dot_general(at_z, at_lane, (((1,), (1,)), ((), ())), preferred_element_type=F32)

    other_targets = pl.multiple_of((1 - core) * depth, depth)
    my_targets = pl.multiple_of(core * depth, depth)
    table_send = send(table.at[pl.ds(other_rows, half)], table_core, core_sem, CHUNKS, to_core)
    target_send = send(target.at[pl.ds(other_targets, depth)], target_got, core_sem, CHUNKS + 1, to_core)
    table_send.start()
    target_send.start()

    x_sends = []
    for ch in range(CHUNKS):
        core_sends[ch].wait()
        part[ch, pl.ds(my_rows, half), :] += core_got[ch]
        copy = send(part.at[ch, pl.ds(other_x, depth)], x_got.at[ch], x_sem, ch, to_x)
        copy.start()
        x_sends.append(copy)
        if ch == 0:
            table_send.wait()
            table[pl.ds(my_rows, half), :] += table_core[...]
            table_x_send = send(table.at[pl.ds(other_x, depth)], table_x, x_sem, CHUNKS, to_x)
            table_x_send.start()

    def along_z(out, got, i, j):
        peer = z_peer(j)
        return pltpu.make_async_remote_copy(
            src_ref=out.at[peer],
            dst_ref=got.at[depth - j],
            send_sem=i[0],
            recv_sem=i[1],
            device_id=at(peer * QUAD + quad, shell),
            device_id_type=MESH,
        )

    def all_of(out, got, i):
        return pltpu.make_async_remote_copy(
            src_ref=out.at[pl.ds(0, depth - 1)],
            dst_ref=got.at[pl.ds(1, depth - 1)],
            send_sem=i[0],
            recv_sem=i[1],
            device_id=at(z_peer(1) * QUAD + quad, shell),
            device_id_type=MESH,
        )

    note_sems = (note_sem.at[0], note_sem.at[1])
    for ch in range(CHUNKS):
        x_sends[ch].wait()
        total = part[ch, pl.ds(my_x, depth), :] + x_got[ch]
        for b in range(2 * RUN):
            stage[ch, :, b, :] = total[:, b * LANES : (b + 1) * LANES]
        z_out[ch] = stage[ch].astype(BF16)

        for j in far_first:
            along_z(z_out.at[ch], z_got.at[ch], (z_sem.at[0, ch], z_sem.at[1, ch]), j).start()
        if ch == 0:
            table_x_send.wait()
            target_send.wait()
            own_table = table[pl.ds(my_x, depth), :] + table_x[...]
            note_out[:, 0, :] = own_table + target[pl.ds(my_targets, depth), :] + pltpu.roll(target_got[...], 4, 1)
            note_got[0] = note_out[z]

            for j in far_first:
                along_z(note_out, note_got, note_sems, j).start()

    all_of(note_out, note_got, note_sems).wait()
    values = note_got[:, 0, :]
    for i in range(QUAD * CAP):
        column[i] = jnp.broadcast_to(values[:, 64 + i : 65 + i], (depth, LANES))

    @pl.loop(0, CHUNKS * RUN)
    def _(k):
        freq = freq_ref[pl.ds(k, 1), :]
        total = jnp.zeros((depth, LANES), F32)
        for i in range(QUAD * CAP):
            s, _ = folded(column[i] * freq)
            total = total + s * s
        power[pl.ds(k, 1), :] = jnp.sum(total, axis=0, keepdims=True)

    across = iota((LANES, LANES), 1)
    slot_of = (across // 64 * 4 + across % 4 == iota((LANES, LANES), 0)).astype(F32).astype(BF16)
    from_z = (iota((depth, LANES), 1) % 64 // 4 == iota((depth, LANES), 0)).astype(F32)
    to_block = jnp.sum(dot(values.astype(BF16), slot_of) * from_z, axis=0, keepdims=True)
    adds[...] = (to_block == (iota((64, LANES), 0) + 1).astype(F32)).astype(F32).astype(BF16)
    terms[...] = jnp.zeros_like(terms)
    coef_load.wait()
    smalls[4].wait()

    for ch in range(CHUNKS):
        all_of(z_out.at[ch], z_got.at[ch], (z_sem.at[0, ch], z_sem.at[1, ch])).wait()
        numerator = stage[ch, z]
        for j in range(1, depth):
            numerator = numerator + z_got[ch, j].astype(F32)
        for c in range(2):
            for q in range(RUN):
                k = ch * RUN + q
                model = model_ref[c : c + 1, k * LANES : (k + 1) * LANES]
                resid[c * 16 + k : c * 16 + k + 1, :] = (
                    power[k : k + 1, :] * model - numerator[c * RUN + q : c * RUN + q + 1, :]
                ) * (1.0 / 128)
        for q in range(RUN):
            k = ch * RUN + q
            left = jnp.concatenate([resid[k : k + 1, :], resid[16 + k : 17 + k, :]], axis=0).astype(BF16)
            for j in range(NNZ):
                term = dot(left, coef[k, j])
                t = j * 16 + k
                terms[t : t + 1, 0:LANES] = term[0:1]
                terms[t : t + 1, LANES : 2 * LANES] = term[1:2]

    high, low = halves(terms[...])
    slots = dot(place[...], high) + dot(place[...], low)
    slot_out[pl.ds(0, LANES, stride=2), :] = slots[:, 0:LANES]
    slot_out[pl.ds(1, LANES, stride=2), :] = slots[:, LANES : 2 * LANES]
    for j in far_first + [0]:
        for other in range(2):
            if j or other:
                side = 1 - core if other else core
                peer = z_peer(j)
                send(
                    slot_out.at[pl.ds(pl.multiple_of((side * depth + peer) * 8, 8), 8)],
                    slot_got.at[pl.ds((other * depth + (depth - j) % depth) * 8, 8)],
                    slot_sem,
                    0,
                    at(peer * QUAD + x_lo * 2 + side, shell),
                ).start()
    slot_got[0:8, :] = slot_out[pl.ds(pl.multiple_of((core * depth + z) * 8, 8), 8), :]
    rest = 8 * (2 * depth - 1)
    send(slot_out.at[pl.ds(0, rest)], slot_got.at[pl.ds(8, rest)], slot_sem, 0, to_core).wait()
    for c in range(2):
        high, low = halves(slot_got[pl.ds(c, LANES, stride=2), :])
        plane_out[pl.ds(c, 64, stride=2), :] = dot(adds[...], high) + dot(adds[...], low)

    for offset in NEAR:
        peer_x, peer_shell = plane_peer(offset)
        spot = NEAR.index((offset[0], -offset[1] % 4, offset[2]))
        send(
            plane_out.at[pl.ds(pl.multiple_of((peer_x * SHELLS + peer_shell) * 8, 8), 8)],
            plane_got.at[pl.ds(spot * 8, 8)],
            plane_sem,
            0,
            at(z * QUAD + peer_x * 2 + core, peer_shell),
        ).start()
    total = plane_out[pl.ds(pl.multiple_of((x_lo * SHELLS + shell) * 8, 8), 8), :]
    rest = 8 * len(NEAR)
    send(plane_out.at[pl.ds(0, rest)], plane_got, plane_sem, 0, to_core).wait()
    for i in range(len(NEAR)):
        total = total + plane_got[i * 8 : i * 8 + 8, :]
    out_ref[...] = total


NNZ = 4
NNZ_ROWS = NNZ


def shards(images, defocus, pose_bin, freq_sq, model_slice, interp_coef, block_index):
    depth = lax.axis_size("slab") // QUAD
    rows, _, width = images.shape
    run = RUN * LANES
    vmem = pl.BlockSpec(memory_space=pltpu.VMEM)
    hbm = pl.BlockSpec(memory_space=pl.ANY)
    dma = pltpu.SemaphoreType.DMA
    out = pl.pallas_call(
        functools.partial(kernel, depth),
        out_shape=jax.ShapeDtypeStruct((8, LANES), F32),
        in_specs=[hbm] * 7,
        out_specs=vmem,
        scratch_shapes=[
            pltpu.VMEM((1, rows), jnp.int32),
            pltpu.VMEM((1, rows), BF16),
            pltpu.VMEM((width // LANES, LANES), F32),
            pltpu.VMEM((2, width), F32),
            pltpu.VMEM((NNZ, 16), jnp.int32),
            pltpu.VMEM((2 * rows, width), BF16),
            pltpu.VMEM(interp_coef.shape[1:], BF16),
            pltpu.VMEM((LANES, LANES), F32),
            pltpu.VMEM((LANES, 2 * LANES), BF16),
            pltpu.VMEM((2 * LANES, LANES), F32),
            pltpu.VMEM((CHUNKS, QUAD * depth, 2 * run), F32),
            pltpu.VMEM((CHUNKS, 2 * depth, 2 * run), F32),
            pltpu.VMEM((CHUNKS, depth, 2 * run), F32),
            pltpu.VMEM((QUAD * depth, LANES), F32),
            pltpu.VMEM((2 * depth, LANES), F32),
            pltpu.VMEM((depth, LANES), F32),
            pltpu.VMEM((CHUNKS, depth, 2 * RUN, LANES), F32),
            pltpu.VMEM((CHUNKS, depth, 2 * RUN, LANES), BF16),
            pltpu.VMEM((CHUNKS, depth, 2 * RUN, LANES), BF16),
            pltpu.VMEM((depth, 1, LANES), F32),
            pltpu.VMEM((depth, 1, LANES), F32),
            pltpu.VMEM((QUAD * CAP, depth, LANES), F32),
            pltpu.VMEM((16, LANES), F32),
            pltpu.VMEM((32, LANES), F32),
            pltpu.VMEM((LANES, LANES), BF16),
            pltpu.VMEM((2 * depth, LANES), F32),
            pltpu.VMEM((depth, LANES), F32),
            pltpu.VMEM((64, LANES), BF16),
            pltpu.VMEM((LANES, 2 * LANES), F32),
            pltpu.VMEM((2 * LANES, LANES), F32),
            pltpu.VMEM((2 * LANES, LANES), F32),
            pltpu.VMEM((PLANE * 8, LANES), F32),
            pltpu.VMEM((len(NEAR) * 8, LANES), F32),
            dma((5,)),
            dma((CHUNKS,)),
            dma,
            dma((2, CHUNKS + 2)),
            dma((2, CHUNKS + 1)),
            dma((2, CHUNKS)),
            dma((2,)),
            dma((2, 1)),
            dma((2, 1)),
        ],
        compiler_params=pltpu.CompilerParams(collective_id=0, has_side_effects=True),
        name="cryo_grad",
    )(
        pose_bin.reshape(1, rows),
        defocus.reshape(1, rows),
        freq_sq.reshape(width // LANES, LANES),
        model_slice[0],
        jnp.transpose(block_index[0]),
        images,
        interp_coef[0],
    )
    return out.reshape(4, 2, LANES)


def solution(mesh):
    return jax.shard_map(
        shards,
        mesh=mesh,
        in_specs=(
            P("slab", None, "shell"),
            P("slab"),
            P("slab", None),
            P("shell"),
            P("slab", None, "shell"),
            P("slab", "shell", None, None, None),
            P("slab", "shell", None),
        ),
        out_specs=P(("slab", "shell"), None, None),
        check_vma=False,
    )
```

time: 55.7 us -> 49.5 us (0.89)
  Pallas kernels: 52 us -> 48.1 us
  local copies, waits for them, and re-layouts: 3.53 us -> 1.28 us
    pallas_call x1, Pallas kernels: 52 us -> 48.1 us  [shards(): pl.pallas_call(functools.partial(kernel, depth), out_shape=jax.ShapeDtype...]
    reshape x1 -> x0, local copies, waits for them, and re-layouts: 2.26 us -> none  [shards(): images.reshape(2 * rows, width)]
where the time goes in v2:
time: 49.5 us; the launch traced here: 49.3 us
  Pallas kernels  48.1 us (97%)
  local copies, waits for them, and re-layouts  1.28 us (3%)
    pallas_call x1, Pallas kernels, shards(): pl.pallas_call(functools.partial(kernel, depth), out_shape=jax.ShapeDtype...  48.1 us
    unnamed x1, local copies, waits for them, and re-layouts  1.28 us

profile of v2, /device:TPU:1, one launch (start us, length us, event | category | flops | bytes accessed | tf_op | source)
XLA Modules:
  0.0 49.3 jit_solution(6616872307051549076)
XLA Ops:
  0.0 48.1 %cryo_grad.1 = f32[8,128]{1,0:T(8,128)} custom-call(s32[1,128]{1,0:T(1,128)} %bitcast.14, bf16[1,128]{1,0:T(2,128)(2,1)} %bitcast.15, f32[16,128]{1,0:T(8,128)} %bitcast.12, f32[2,2048]{1,0:T(2,128)} %bitcast.10, s32[4,16]{1,0:T(4,128)} %bitcast.13, bf16[128,2,2048]{2,1,0:T(2,128)(2,1)} %images_ref.1, bf16[16,4,128,128]{3,2,1,0:T(8,128)(2,1)} %bitcast.9), custom_call_target="tpu_custom_call" | custom-call | tf_op jit(solution)/shard_map/cryo_grad/pallas_call | solution.py:415
  48.1 1.3 %copy.9 = f32[4,2,128]{2,1,0:T(2,128)} copy(f32[4,2,128]{2,1,0:T(2,128)} %bitcast.11) | data formatting | bytes 8192

commit v3 on v2

--- a/solution.py
+++ b/solution.py
@@ -99,6 +99,7 @@
     slot_got,
     plane_out,
     plane_got,
+    far_sem,
     small_sem,
     img_sem,
     coef_sem,
@@ -155,11 +156,10 @@
     barrier = pltpu.get_barrier_semaphore()
 
     far_first = sorted(range(1, depth), key=lambda j: -min(j, depth - j))
-    for j in far_first:
-        for side in (core, 1 - core):
-            pl.semaphore_signal(
-                barrier, inc=1, device_id=at(z_peer(j) * QUAD + x_lo * 2 + side, shell), device_id_type=MESH
-            )
+    reach = depth // 4
+    close = [j for j in far_first if min(j, depth - j) <= reach]
+    for j in close:
+        pl.semaphore_signal(barrier, inc=1, device_id=at(z_peer(j) * QUAD + quad, shell), device_id_type=MESH)
 
     for offset in NEAR:
         peer_x, peer_shell = plane_peer(offset)
@@ -183,8 +183,25 @@
         ((bin64.astype(F32) == pose_pair) & (parity == wide // 64)).astype(F32).astype(BF16)
     )
 
-    smalls[2].wait()
-    for ch in range(CHUNKS):
+    half = 2 * depth
+    other_rows = pl.multiple_of((1 - core) * half, half)
+    my_rows = pl.multiple_of(core * half, half)
+    other_x = pl.multiple_of(core * half + (1 - x_lo) * depth, depth)
+    my_x = pl.multiple_of(core * half + x_lo * depth, depth)
+
+    def send(src, dst, sems, i, device):
+        return pltpu.make_async_remote_copy(
+            src_ref=src,
+            dst_ref=dst,
+            send_sem=sems.at[0, i],
+            recv_sem=sems.at[1, i],
+            device_id=device,
+            device_id_type=MESH,
+        )
+
+    to_core = at(core_peer, shell)
+    to_x = at(x_peer, shell)
+    def summed(ch):
         loads[ch].wait()
 
         @pl.loop(0, RUN)
@@ -200,31 +217,24 @@
             part[ch, :, pl.ds(first, LANES)] = sums[0:64]
             part[ch, :, pl.ds(pl.multiple_of(width + first, LANES), LANES)] = sums[64:128]
 
-    pl.semaphore_wait(barrier, 2 * (depth - 1) + len(NEAR) + 1)
-
-    half = 2 * depth
-    other_rows = pl.multiple_of((1 - core) * half, half)
-    my_rows = pl.multiple_of(core * half, half)
-    other_x = pl.multiple_of(core * half + (1 - x_lo) * depth, depth)
-    my_x = pl.multiple_of(core * half + x_lo * depth, depth)
-
-    def send(src, dst, sems, i, device):
-        return pltpu.make_async_remote_copy(
-            src_ref=src,
-            dst_ref=dst,
-            send_sem=sems.at[0, i],
-            recv_sem=sems.at[1, i],
-            device_id=device,
-            device_id_type=MESH,
-        )
-
-    to_core = at(core_peer, shell)
-    to_x = at(x_peer, shell)
     core_sends = [
         send(part.at[ch, pl.ds(other_rows, half)], core_got.at[ch], core_sem, ch, to_core) for ch in range(CHUNKS)
     ]
-    for copy in core_sends:
-        copy.start()
+    x_sends = [
+        send(part.at[ch, pl.ds(other_x, depth)], x_got.at[ch], x_sem, ch, to_x) for ch in range(CHUNKS)
+    ]
+
+    def pass_on(ch):
+        core_sends[ch].wait()
+        part[ch, pl.ds(my_rows, half), :] += core_got[ch]
+        x_sends[ch].start()
+
+    smalls[2].wait()
+    summed(0)
+    pl.semaphore_wait(barrier, len(close) + len(NEAR) + 1)
+    core_sends[0].start()
+    for j in (reach, depth - reach):
+        pl.semaphore_signal(far_sem, inc=1, device_id=at(z_peer(j) * QUAD + quad, shell), device_id_type=MESH)
 
     same = (pose_col == pose) & (iota((LANES, LANES), 1) < iota((LANES, LANES), 0))
     rank = jnp.sum(same.astype(F32), axis=1, keepdims=True)
@@ -262,18 +272,17 @@
     table_send.start()
     target_send.start()
 
-    x_sends = []
-    for ch in range(CHUNKS):
-        core_sends[ch].wait()
-        part[ch, pl.ds(my_rows, half), :] += core_got[ch]
-        copy = send(part.at[ch, pl.ds(other_x, depth)], x_got.at[ch], x_sem, ch, to_x)
-        copy.start()
-        x_sends.append(copy)
-        if ch == 0:
+    table_x_send = send(table.at[pl.ds(other_x, depth)], table_x, x_sem, CHUNKS, to_x)
+    for ch in range(1, CHUNKS):
+        summed(ch)
+        core_sends[ch].start()
+        if ch == 2:
+            pass_on(0)
             table_send.wait()
             table[pl.ds(my_rows, half), :] += table_core[...]
-            table_x_send = send(table.at[pl.ds(other_x, depth)], table_x, x_sem, CHUNKS, to_x)
             table_x_send.start()
+    for ch in range(1, CHUNKS):
+        pass_on(ch)
 
     def along_z(out, got, i, j):
         peer = z_peer(j)
@@ -297,6 +306,7 @@
         )
 
     note_sems = (note_sem.at[0], note_sem.at[1])
+    pl.semaphore_wait(far_sem, 2)
     for ch in range(CHUNKS):
         x_sends[ch].wait()
         total = part[ch, pl.ds(my_x, depth), :] + x_got[ch]
@@ -451,6 +461,7 @@
             pltpu.VMEM((2 * LANES, LANES), F32),
             pltpu.VMEM((PLANE * 8, LANES), F32),
             pltpu.VMEM((len(NEAR) * 8, LANES), F32),
+            pltpu.SemaphoreType.REGULAR,
             dma((5,)),
             dma((CHUNKS,)),
             dma,
@@ -461,9 +472,9 @@
             dma((2, 1)),
             dma((2, 1)),
         ],
-        compiler_params=pltpu.CompilerParams(collective_id=0, has_side_effects=True),
+        compiler_params=pltpu.CompilerParams(collective_id=0, has_side_effects=True, vmem_limit_bytes=20 << 20),
         name="cryo_grad",
-    )(
+    )(*(pltpu.with_memory_space_constraint(a, pltpu.HBM) for a in (
         pose_bin.reshape(1, rows),
         defocus.reshape(1, rows),
         freq_sq.reshape(width // LANES, LANES),
@@ -471,7 +482,7 @@
         jnp.transpose(block_index[0]),
         images,
         interp_coef[0],
-    )
+    )))
     return out.reshape(4, 2, LANES)
 
 

time: 49.5 us -> 46.4 us (0.937)
  Pallas kernels: 48.1 us -> 45.7 us
  local copies, waits for them, and re-layouts: 1.28 us -> 0.6 us
    pallas_call x1, Pallas kernels: 48.1 us -> 45.7 us  [shards(): pl.pallas_call(functools.partial(kernel, depth), out_shape=jax.ShapeDtype...]
    unnamed x1, local copies, waits for them, and re-layouts: 1.28 us -> 0.6 us
where the time goes in v3:
time: 46.4 us; the launch traced here: 46.3 us
  Pallas kernels  45.7 us (98%)
  local copies, waits for them, and re-layouts  0.6 us (1%)
    pallas_call x1, Pallas kernels, shards(): pl.pallas_call(functools.partial(kernel, depth), out_shape=jax.ShapeDtype...  45.7 us

profile of v3, /device:TPU:1, one launch (start us, length us, event | category | flops | bytes accessed | tf_op | source)
XLA Modules:
  0.0 46.3 jit_solution(8007730791087262608)
XLA Ops:
  0.0 45.7 %cryo_grad.1 = f32[8,128]{1,0:T(8,128)S(1)} custom-call(s32[1,128]{1,0:T(1,128)} %bitcast.14, bf16[1,128]{1,0:T(2,128)(2,1)} %bitcast.15, f32[16,128]{1,0:T(8,128)} %bitcast.12, f32[2,2048]{1,0:T(2,128)} %bitcast.11, s32[4,16]{1,0:T(4,128)} %bitcast.13, bf16[128,2,2048]{2,1,0:T(2,128)(2,1)} %images_ref.1, bf16[16,4,128,128]{3,2,1,0:T(8,128)(2,1)} %bitcast.10), custom_call_target="tpu_custom_call" | custom-call | tf_op jit(solution)/shard_map/cryo_grad/pallas_call | solution.py:425
  45.7 0.6 %copy.9 = f32[4,2,128]{2,1,0:T(2,128)} copy(f32[4,2,128]{2,1,0:T(2,128)S(1)} %bitcast.9) | data formatting | bytes 8192

commit v4 on v3

--- a/solution.py
+++ b/solution.py
@@ -15,8 +15,10 @@
 SHELLS = 8
 CAP = 6
 LANES = 128
-CHUNKS = 4
-RUN = 4
+RUNS = (4, 4, 4, 4)
+STARTS = tuple(sum(RUNS[:i]) for i in range(len(RUNS)))
+CHUNKS = len(RUNS)
+EARLY = (4, 12, 3, 13, 2, 14, 1, 15)
 NEAR = [(dx, dy, dh) for dx in range(2) for dy in range(4) for dh in range(2)]
 NEAR = sorted(NEAR, key=lambda d: -(min(d[1], 4 - d[1]) + abs(2 * d[2] - d[0])))[:-1]
 PLANE = 16
@@ -128,13 +130,14 @@
         dx, dy, dh = offset
         return (x_lo + dx) % 2, (y + dy) % 4 * 2 + (x_hi + dh) % 2
 
-    width = RUN * LANES
     rows_ref = images_ref.reshape(2 * images_ref.shape[0], images_ref.shape[2])
     loads = [
         pltpu.make_async_copy(
-            rows_ref.at[:, pl.ds(ch * width, width)], img.at[:, pl.ds(ch * width, width)], img_sem.at[ch]
+            rows_ref.at[:, pl.ds(start * LANES, run * LANES)],
+            img.at[:, pl.ds(start * LANES, run * LANES)],
+            img_sem.at[ch],
         )
-        for ch in range(CHUNKS)
+        for ch, (start, run) in enumerate(zip(STARTS, RUNS))
     ]
     smalls = [
         pltpu.make_async_copy(src, dst, small_sem.at[i])
@@ -204,9 +207,9 @@
     def summed(ch):
         loads[ch].wait()
 
-        @pl.loop(0, RUN)
+        @pl.loop(0, RUNS[ch])
         def _(q):
-            k = ch * RUN + q
+            k = STARTS[ch] + q
             contrast = sine(focus_col[...] * freq_ref[pl.ds(k, 1), :])
             spread[pl.ds(0, LANES, stride=2), :] = contrast
             spread[pl.ds(1, LANES, stride=2), :] = contrast
@@ -214,19 +217,20 @@
             high, low = halves(spread[...] * picture)
             sums = dot(pair_hot[...], high) + dot(pair_hot[...], low)
             first = pl.multiple_of(q * LANES, LANES)
-            part[ch, :, pl.ds(first, LANES)] = sums[0:64]
-            part[ch, :, pl.ds(pl.multiple_of(width + first, LANES), LANES)] = sums[64:128]
+            second = pl.multiple_of(RUNS[ch] * LANES + first, LANES)
+            part[ch][:, pl.ds(first, LANES)] = sums[0:64]
+            part[ch][:, pl.ds(second, LANES)] = sums[64:128]
 
     core_sends = [
-        send(part.at[ch, pl.ds(other_rows, half)], core_got.at[ch], core_sem, ch, to_core) for ch in range(CHUNKS)
+        send(part[ch].at[pl.ds(other_rows, half)], core_got[ch], core_sem, ch, to_core) for ch in range(CHUNKS)
     ]
     x_sends = [
-        send(part.at[ch, pl.ds(other_x, depth)], x_got.at[ch], x_sem, ch, to_x) for ch in range(CHUNKS)
+        send(part[ch].at[pl.ds(other_x, depth)], x_got[ch], x_sem, ch, to_x) for ch in range(CHUNKS)
     ]
 
     def pass_on(ch):
         core_sends[ch].wait()
-        part[ch, pl.ds(my_rows, half), :] += core_got[ch]
+        part[ch][pl.ds(my_rows, half), :] += core_got[ch][...]
         x_sends[ch].start()
 
     smalls[2].wait()
@@ -276,7 +280,7 @@
     for ch in range(1, CHUNKS):
         summed(ch)
         core_sends[ch].start()
-        if ch == 2:
+        if ch == 1:
             pass_on(0)
             table_send.wait()
             table[pl.ds(my_rows, half), :] += table_core[...]
@@ -306,32 +310,37 @@
         )
 
     note_sems = (note_sem.at[0], note_sem.at[1])
-    pl.semaphore_wait(far_sem, 2)
+
+    def z_send(ch, to):
+        for j in to:
+            along_z(z_out[ch], z_got[ch], (z_sem.at[0, ch], z_sem.at[1, ch]), j).start()
+
     for ch in range(CHUNKS):
         x_sends[ch].wait()
-        total = part[ch, pl.ds(my_x, depth), :] + x_got[ch]
-        for b in range(2 * RUN):
-            stage[ch, :, b, :] = total[:, b * LANES : (b + 1) * LANES]
-        z_out[ch] = stage[ch].astype(BF16)
+        total = part[ch][pl.ds(my_x, depth), :] + x_got[ch][...]
+        for b in range(2 * RUNS[ch]):
+            stage[ch][:, b, :] = total[:, b * LANES : (b + 1) * LANES]
+        z_out[ch][...] = stage[ch][...].astype(BF16)
+        if ch > 0:
+            z_send(ch, far_first)
+            continue
+        z_send(0, EARLY)
+        pl.semaphore_wait(far_sem, 2)
+        z_send(0, [j for j in far_first if j not in EARLY])
+        table_x_send.wait()
+        target_send.wait()
+        own_table = table[pl.ds(my_x, depth), :] + table_x[...]
+        note_out[:, 0, :] = own_table + target[pl.ds(my_targets, depth), :] + pltpu.roll(target_got[...], 4, 1)
+        note_got[0] = note_out[z]
 
         for j in far_first:
-            along_z(z_out.at[ch], z_got.at[ch], (z_sem.at[0, ch], z_sem.at[1, ch]), j).start()
-        if ch == 0:
-            table_x_send.wait()
-            target_send.wait()
-            own_table = table[pl.ds(my_x, depth), :] + table_x[...]
-            note_out[:, 0, :] = own_table + target[pl.ds(my_targets, depth), :] + pltpu.roll(target_got[...], 4, 1)
-            note_got[0] = note_out[z]
-
-            for j in far_first:
-                along_z(note_out, note_got, note_sems, j).start()
-
+            along_z(note_out, note_got, note_sems, j).start()
     all_of(note_out, note_got, note_sems).wait()
     values = note_got[:, 0, :]
     for i in range(QUAD * CAP):
         column[i] = jnp.broadcast_to(values[:, 64 + i : 65 + i], (depth, LANES))
 
-    @pl.loop(0, CHUNKS * RUN)
+    @pl.loop(0, sum(RUNS))
     def _(k):
         freq = freq_ref[pl.ds(k, 1), :]
         total = jnp.zeros((depth, LANES), F32)
@@ -350,19 +359,19 @@
     smalls[4].wait()
 
     for ch in range(CHUNKS):
-        all_of(z_out.at[ch], z_got.at[ch], (z_sem.at[0, ch], z_sem.at[1, ch])).wait()
-        numerator = stage[ch, z]
+        all_of(z_out[ch], z_got[ch], (z_sem.at[0, ch], z_sem.at[1, ch])).wait()
+        numerator = stage[ch][z]
         for j in range(1, depth):
-            numerator = numerator + z_got[ch, j].astype(F32)
+            numerator = numerator + z_got[ch][j].astype(F32)
         for c in range(2):
-            for q in range(RUN):
-                k = ch * RUN + q
+            for q in range(RUNS[ch]):
+                k = STARTS[ch] + q
                 model = model_ref[c : c + 1, k * LANES : (k + 1) * LANES]
                 resid[c * 16 + k : c * 16 + k + 1, :] = (
-                    power[k : k + 1, :] * model - numerator[c * RUN + q : c * RUN + q + 1, :]
+                    power[k : k + 1, :] * model - numerator[c * RUNS[ch] + q : c * RUNS[ch] + q + 1, :]
                 ) * (1.0 / 128)
-        for q in range(RUN):
-            k = ch * RUN + q
+        for q in range(RUNS[ch]):
+            k = STARTS[ch] + q
             left = jnp.concatenate([resid[k : k + 1, :], resid[16 + k : 17 + k, :]], axis=0).astype(BF16)
             for j in range(NNZ):
                 term = dot(left, coef[k, j])
@@ -418,7 +427,6 @@
 def shards(images, defocus, pose_bin, freq_sq, model_slice, interp_coef, block_index):
     depth = lax.axis_size("slab") // QUAD
     rows, _, width = images.shape
-    run = RUN * LANES
     vmem = pl.BlockSpec(memory_space=pltpu.VMEM)
     hbm = pl.BlockSpec(memory_space=pl.ANY)
     dma = pltpu.SemaphoreType.DMA
@@ -438,15 +446,15 @@
             pltpu.VMEM((LANES, LANES), F32),
             pltpu.VMEM((LANES, 2 * LANES), BF16),
             pltpu.VMEM((2 * LANES, LANES), F32),
-            pltpu.VMEM((CHUNKS, QUAD * depth, 2 * run), F32),
-            pltpu.VMEM((CHUNKS, 2 * depth, 2 * run), F32),
-            pltpu.VMEM((CHUNKS, depth, 2 * run), F32),
+            [pltpu.VMEM((QUAD * depth, 2 * run * LANES), F32) for run in RUNS],
+            [pltpu.VMEM((2 * depth, 2 * run * LANES), F32) for run in RUNS],
+            [pltpu.VMEM((depth, 2 * run * LANES), F32) for run in RUNS],
             pltpu.VMEM((QUAD * depth, LANES), F32),
             pltpu.VMEM((2 * depth, LANES), F32),
             pltpu.VMEM((depth, LANES), F32),
-            pltpu.VMEM((CHUNKS, depth, 2 * RUN, LANES), F32),
-            pltpu.VMEM((CHUNKS, depth, 2 * RUN, LANES), BF16),
-            pltpu.VMEM((CHUNKS, depth, 2 * RUN, LANES), BF16),
+            [pltpu.VMEM((depth, 2 * run, LANES), F32) for run in RUNS],
+            [pltpu.VMEM((depth, 2 * run, LANES), BF16) for run in RUNS],
+            [pltpu.VMEM((depth, 2 * run, LANES), BF16) for run in RUNS],
             pltpu.VMEM((depth, 1, LANES), F32),
             pltpu.VMEM((depth, 1, LANES), F32),
             pltpu.VMEM((QUAD * CAP, depth, LANES), F32),

time: 46.4 us -> 46.2 us (level)
  no operation moved by 1% of the time
where the time goes in v4:
time: 46.2 us; the launch traced here: 46.1 us
  Pallas kernels  45.4 us (98%)
  local copies, waits for them, and re-layouts  0.6 us (1%)
    pallas_call x1, Pallas kernels, shards(): pl.pallas_call(functools.partial(kernel, depth), out_shape=jax.ShapeDtype...  45.4 us

profile of v4, /device:TPU:1, one launch (start us, length us, event | category | flops | bytes accessed | tf_op | source)
XLA Modules:
  0.0 46.1 jit_solution(10147828738793493279)
XLA Ops:
  0.0 45.4 %cryo_grad.1 = f32[8,128]{1,0:T(8,128)S(1)} custom-call(s32[1,128]{1,0:T(1,128)} %bitcast.14, bf16[1,128]{1,0:T(2,128)(2,1)} %bitcast.15, f32[16,128]{1,0:T(8,128)} %bitcast.12, f32[2,2048]{1,0:T(2,128)} %bitcast.11, s32[4,16]{1,0:T(4,128)} %bitcast.13, bf16[128,2,2048]{2,1,0:T(2,128)(2,1)} %images_ref.1, bf16[16,4,128,128]{3,2,1,0:T(8,128)(2,1)} %bitcast.10), custom_call_target="tpu_custom_call" | custom-call | tf_op jit(solution)/shard_map/cryo_grad/pallas_call | solution.py:433
  45.5 0.6 %copy.9 = f32[4,2,128]{2,1,0:T(2,128)} copy(f32[4,2,128]{2,1,0:T(2,128)S(1)} %bitcast.9) | data formatting | bytes 8192

commit v5 on v4

--- a/solution.py
+++ b/solution.py
@@ -80,6 +80,7 @@
     spread,
     part,
     core_got,
+    x_out,
     x_got,
     table,
     table_core,
@@ -97,6 +98,7 @@
     target_got,
     adds,
     terms,
+    slot_stage,
     slot_out,
     slot_got,
     plane_out,
@@ -204,6 +206,7 @@
 
     to_core = at(core_peer, shell)
     to_x = at(x_peer, shell)
+
     def summed(ch):
         loads[ch].wait()
 
@@ -225,12 +228,13 @@
         send(part[ch].at[pl.ds(other_rows, half)], core_got[ch], core_sem, ch, to_core) for ch in range(CHUNKS)
     ]
     x_sends = [
-        send(part[ch].at[pl.ds(other_x, depth)], x_got[ch], x_sem, ch, to_x) for ch in range(CHUNKS)
+        send(x_out[ch], x_got[ch], x_sem, ch, to_x) for ch in range(CHUNKS)
     ]
 
     def pass_on(ch):
         core_sends[ch].wait()
         part[ch][pl.ds(my_rows, half), :] += core_got[ch][...]
+        x_out[ch][...] = part[ch][pl.ds(other_x, depth), :].astype(BF16)
         x_sends[ch].start()
 
     smalls[2].wait()
@@ -317,7 +321,7 @@
 
     for ch in range(CHUNKS):
         x_sends[ch].wait()
-        total = part[ch][pl.ds(my_x, depth), :] + x_got[ch][...]
+        total = part[ch][pl.ds(my_x, depth), :] + x_got[ch][...].astype(F32)
         for b in range(2 * RUNS[ch]):
             stage[ch][:, b, :] = total[:, b * LANES : (b + 1) * LANES]
         z_out[ch][...] = stage[ch][...].astype(BF16)
@@ -381,26 +385,27 @@
 
     high, low = halves(terms[...])
     slots = dot(place[...], high) + dot(place[...], low)
-    slot_out[pl.ds(0, LANES, stride=2), :] = slots[:, 0:LANES]
-    slot_out[pl.ds(1, LANES, stride=2), :] = slots[:, LANES : 2 * LANES]
+    slot_stage[pl.ds(0, LANES, stride=2), :] = slots[:, 0:LANES]
+    slot_stage[pl.ds(1, LANES, stride=2), :] = slots[:, LANES : 2 * LANES]
+    slot_out[...] = slot_stage[...].reshape(2 * depth, 8, LANES).astype(BF16)
     for j in far_first + [0]:
         for other in range(2):
             if j or other:
                 side = 1 - core if other else core
                 peer = z_peer(j)
                 send(
-                    slot_out.at[pl.ds(pl.multiple_of((side * depth + peer) * 8, 8), 8)],
-                    slot_got.at[pl.ds((other * depth + (depth - j) % depth) * 8, 8)],
+                    slot_out.at[side * depth + peer],
+                    slot_got.at[other * depth + (depth - j) % depth],
                     slot_sem,
                     0,
                     at(peer * QUAD + x_lo * 2 + side, shell),
                 ).start()
-    slot_got[0:8, :] = slot_out[pl.ds(pl.multiple_of((core * depth + z) * 8, 8), 8), :]
-    rest = 8 * (2 * depth - 1)
-    send(slot_out.at[pl.ds(0, rest)], slot_got.at[pl.ds(8, rest)], slot_sem, 0, to_core).wait()
+    slot_got[0] = slot_out[core * depth + z]
+    rest = 2 * depth - 1
+    send(slot_out.at[pl.ds(0, rest)], slot_got.at[pl.ds(1, rest)], slot_sem, 0, to_core).wait()
+    slot_stage[...] = slot_got[...].astype(F32).reshape(2 * LANES, LANES)
     for c in range(2):
-        high, low = halves(slot_got[pl.ds(c, LANES, stride=2), :])
-        plane_out[pl.ds(c, 64, stride=2), :] = dot(adds[...], high) + dot(adds[...], low)
+        plane_out[pl.ds(c, 64, stride=2), :] = dot(adds[...], slot_stage[pl.ds(c, LANES, stride=2), :].astype(BF16))
 
     for offset in NEAR:
         peer_x, peer_shell = plane_peer(offset)
@@ -448,7 +453,8 @@
             pltpu.VMEM((2 * LANES, LANES), F32),
             [pltpu.VMEM((QUAD * depth, 2 * run * LANES), F32) for run in RUNS],
             [pltpu.VMEM((2 * depth, 2 * run * LANES), F32) for run in RUNS],
-            [pltpu.VMEM((depth, 2 * run * LANES), F32) for run in RUNS],
+            [pltpu.VMEM((depth, 2 * run * LANES), BF16) for run in RUNS],
+            [pltpu.VMEM((depth, 2 * run * LANES), BF16) for run in RUNS],
             pltpu.VMEM((QUAD * depth, LANES), F32),
             pltpu.VMEM((2 * depth, LANES), F32),
             pltpu.VMEM((depth, LANES), F32),
@@ -466,7 +472,8 @@
             pltpu.VMEM((64, LANES), BF16),
             pltpu.VMEM((LANES, 2 * LANES), F32),
             pltpu.VMEM((2 * LANES, LANES), F32),
-            pltpu.VMEM((2 * LANES, LANES), F32),
+            pltpu.VMEM((2 * depth, 8, LANES), BF16),
+            pltpu.VMEM((2 * depth, 8, LANES), BF16),
             pltpu.VMEM((PLANE * 8, LANES), F32),
             pltpu.VMEM((len(NEAR) * 8, LANES), F32),
             pltpu.SemaphoreType.REGULAR,

time: 46.2 us -> 44.5 us (0.963)
  Pallas kernels: 45.4 us -> 43.8 us
    pallas_call x1, Pallas kernels: 45.4 us -> 43.8 us  [shards(): pl.pallas_call(functools.partial(kernel, depth), out_shape=jax.ShapeDtype...]
where the time goes in v5:
time: 44.5 us; the launch traced here: 44.4 us
  Pallas kernels  43.8 us (98%)
  local copies, waits for them, and re-layouts  0.6 us (1%)
    pallas_call x1, Pallas kernels, shards(): pl.pallas_call(functools.partial(kernel, depth), out_shape=jax.ShapeDtype...  43.8 us

profile of v5, /device:TPU:1, one launch (start us, length us, event | category | flops | bytes accessed | tf_op | source)
XLA Modules:
  0.0 44.4 jit_solution(10029485906032153041)
XLA Ops:
  0.0 43.8 %cryo_grad.1 = f32[8,128]{1,0:T(8,128)S(1)} custom-call(s32[1,128]{1,0:T(1,128)} %bitcast.14, bf16[1,128]{1,0:T(2,128)(2,1)} %bitcast.15, f32[16,128]{1,0:T(8,128)} %bitcast.12, f32[2,2048]{1,0:T(2,128)} %bitcast.11, s32[4,16]{1,0:T(4,128)} %bitcast.13, bf16[128,2,2048]{2,1,0:T(2,128)(2,1)} %images_ref.1, bf16[16,4,128,128]{3,2,1,0:T(8,128)(2,1)} %bitcast.10), custom_call_target="tpu_custom_call" | custom-call | tf_op jit(solution)/shard_map/cryo_grad/pallas_call | solution.py:438
  43.8 0.6 %copy.9 = f32[4,2,128]{2,1,0:T(2,128)} copy(f32[4,2,128]{2,1,0:T(2,128)S(1)} %bitcast.9) | data formatting | bytes 8192

commit v6 on v5

--- a/solution.py
+++ b/solution.py
@@ -210,19 +210,17 @@
     def summed(ch):
         loads[ch].wait()
 
-        @pl.loop(0, RUNS[ch])
-        def _(q):
+        for q in range(RUNS[ch]):
             k = STARTS[ch] + q
-            contrast = sine(focus_col[...] * freq_ref[pl.ds(k, 1), :])
-            spread[pl.ds(0, LANES, stride=2), :] = contrast
-            spread[pl.ds(1, LANES, stride=2), :] = contrast
-            picture = img[:, pl.ds(pl.multiple_of(k * LANES, LANES), LANES)].astype(F32)
-            high, low = halves(spread[...] * picture)
+            contrast = sine(focus_col[...] * freq_ref[k : k + 1, :])
+            spread[q, pl.ds(0, LANES, stride=2), :] = contrast
+            spread[q, pl.ds(1, LANES, stride=2), :] = contrast
+            picture = img[:, k * LANES : (k + 1) * LANES].astype(F32)
+            high, low = halves(spread[q] * picture)
             sums = dot(pair_hot[...], high) + dot(pair_hot[...], low)
-            first = pl.multiple_of(q * LANES, LANES)
-            second = pl.multiple_of(RUNS[ch] * LANES + first, LANES)
-            part[ch][:, pl.ds(first, LANES)] = sums[0:64]
-            part[ch][:, pl.ds(second, LANES)] = sums[64:128]
+            second = RUNS[ch] + q
+            part[ch][:, q * LANES : (q + 1) * LANES] = sums[0:64]
+            part[ch][:, second * LANES : (second + 1) * LANES] = sums[64:128]
 
     core_sends = [
         send(part[ch].at[pl.ds(other_rows, half)], core_got[ch], core_sem, ch, to_core) for ch in range(CHUNKS)
@@ -284,12 +282,14 @@
     for ch in range(1, CHUNKS):
         summed(ch)
         core_sends[ch].start()
+        if ch == 2:
+            pass_on(1)
         if ch == 1:
             pass_on(0)
             table_send.wait()
             table[pl.ds(my_rows, half), :] += table_core[...]
             table_x_send.start()
-    for ch in range(1, CHUNKS):
+    for ch in range(2, CHUNKS):
         pass_on(ch)
 
     def along_z(out, got, i, j):
@@ -450,7 +450,7 @@
             pltpu.VMEM(interp_coef.shape[1:], BF16),
             pltpu.VMEM((LANES, LANES), F32),
             pltpu.VMEM((LANES, 2 * LANES), BF16),
-            pltpu.VMEM((2 * LANES, LANES), F32),
+            pltpu.VMEM((max(RUNS), 2 * LANES, LANES), F32),
             [pltpu.VMEM((QUAD * depth, 2 * run * LANES), F32) for run in RUNS],
             [pltpu.VMEM((2 * depth, 2 * run * LANES), F32) for run in RUNS],
             [pltpu.VMEM((depth, 2 * run * LANES), BF16) for run in RUNS],

time: 44.5 us -> 43.7 us (0.982)
  Pallas kernels: 43.8 us -> 42.9 us
    pallas_call x1, Pallas kernels: 43.8 us -> 42.9 us  [shards(): pl.pallas_call(functools.partial(kernel, depth), out_shape=jax.ShapeDtype...]
where the time goes in v6:
time: 43.7 us; the launch traced here: 43.5 us
  Pallas kernels  42.9 us (98%)
  local copies, waits for them, and re-layouts  0.6 us (1%)
    pallas_call x1, Pallas kernels, shards(): pl.pallas_call(functools.partial(kernel, depth), out_shape=jax.ShapeDtype...  42.9 us

profile of v6, /device:TPU:1, one launch (start us, length us, event | category | flops | bytes accessed | tf_op | source)
XLA Modules:
  0.0 43.5 jit_solution(12175427820877286874)
XLA Ops:
  0.0 42.9 %cryo_grad.1 = f32[8,128]{1,0:T(8,128)S(1)} custom-call(s32[1,128]{1,0:T(1,128)} %bitcast.14, bf16[1,128]{1,0:T(2,128)(2,1)} %bitcast.15, f32[16,128]{1,0:T(8,128)} %bitcast.12, f32[2,2048]{1,0:T(2,128)} %bitcast.11, s32[4,16]{1,0:T(4,128)} %bitcast.13, bf16[128,2,2048]{2,1,0:T(2,128)(2,1)} %images_ref.1, bf16[16,4,128,128]{3,2,1,0:T(8,128)(2,1)} %bitcast.10), custom_call_target="tpu_custom_call" | custom-call | tf_op jit(solution)/shard_map/cryo_grad/pallas_call | solution.py:438
  43.0 0.6 %copy.9 = f32[4,2,128]{2,1,0:T(2,128)} copy(f32[4,2,128]{2,1,0:T(2,128)S(1)} %bitcast.9) | data formatting | bytes 8192
